TPU v7x, 128 devices: a whole 4x4x4 slice. The times are simulated.
128 devices in a mesh: dp: 16 (over z, x), expert: 8 (over y, core).
Axes of the slice: x: 4, y: 4, z: 4, core: 2. Of those that a mesh axis runs over, the one named last changes fastest.
Arguments:
- tokens: bfloat16 [16384, 1280], P(('dp', 'expert')), may hold values from -6 to 6
- routes: int32 [16384, 2], P(('dp', 'expert')), may hold values from 0 to 31, all different within a row; in each aligned block of 128 rows (0 to 127, 128 to 255, ...) at most 10 rows name the same one
- combine: float32 [16384, 2], P(('dp', 'expert')), may hold values from 0.1 to 1
- w_in: bfloat16 [1280, 163840], P(None, ('dp', 'expert')), may hold values from -0.15625 to 0.15625
- w_out: bfloat16 [163840, 1280], P(('dp', 'expert')), may hold values from -0.078125 to 0.078125
- out_grad: bfloat16 [16384, 1280], P(('dp', 'expert')), may hold values from -6 to 6
- head_w: bfloat16 [1280, 17408], P(None, 'expert'), may hold values from -0.5 to 0.5
- labels: int32 [64, 4], P('dp'), may hold values from 0 to 17407
Outputs:
- mixed_out: bfloat16 [16384, 1280], P(('dp', 'expert'))
- d_tokens: bfloat16 [16384, 1280], P(('dp', 'expert'))
- d_combine: float32 [16384, 2], P(('dp', 'expert'))
- d_w_in: bfloat16 [1280, 163840], P(None, ('dp', 'expert'))
- d_w_out: bfloat16 [163840, 1280], P(('dp', 'expert'))
- image_loss: float32 [64], P('dp')
- d_pooled: float32 [64, 1280], P('dp')
- d_head: bfloat16 [1280, 17408], P('dp', 'expert')
Inputs may be any that keep to these rules, and one draw needn't show every extreme that they name: `routes`: in the 128 rows of each device no expert is named by more than 10 rows, a bound that some block reaches; the two entries of a row differ. `labels`: entries of one image may repeat.
All inputs are finite; a program needn't handle non-finite values.
Results may differ from a plain program's by a relative error of at most 0.015.
Values may be sent and summed in bfloat16 or wider, within the bound.
No kernel may reach another device: no remote copies, remote signals or barrier semaphores. Data moves between devices by JAX's collectives and lax.ppermute only.
A program may use at most 192 MiB of HBM per device.

v0:
```python
import jax
import jax.numpy as jnp
from jax import lax
from jax.sharding import PartitionSpec as P

D = 1280
EXPERTS = 32
PATCHES = 256
CLASSES = 17408
beta_rate = 0.99
norm_eps = 1e-06


def gelu_fn(values):
    return jax.nn.gelu(values, approximate=True)


def normalize(pooled):
    center = jnp.mean(pooled, axis=1, keepdims=True)
    spread = jnp.mean(jnp.square(pooled - center), axis=1, keepdims=True)
    return (pooled - center) * lax.rsqrt(spread + norm_eps)


def weighted_focal(logit_vals, targets, class_weight):
    nll_vals = targets * jax.nn.softplus(-logit_vals) + (1.0 - targets) * jax.nn.softplus(
        logit_vals
    )
    return class_weight[None, :] * jnp.square(1.0 - jnp.exp(-nll_vals)) * nll_vals


def expert_pass(xs_rows, grad_rows, w_first, w_second):
    h_pre = jnp.dot(xs_rows, w_first, preferred_element_type=jnp.float32)
    hidden, gelu_back = jax.vjp(gelu_fn, h_pre)
    hidden_bf = hidden.astype(jnp.bfloat16)
    expert_out = jnp.dot(hidden_bf, w_second, preferred_element_type=jnp.float32)
    d_hidden = lax.dot_general(
        grad_rows, w_second, (((1,), (1,)), ((), ())), preferred_element_type=jnp.float32
    )
    d_pre = gelu_back(d_hidden)[0].astype(jnp.bfloat16)
    d_second = lax.dot_general(
        hidden_bf, grad_rows, (((0,), (0,)), ((), ())), preferred_element_type=jnp.float32
    ).astype(jnp.bfloat16)
    d_first = lax.dot_general(
        xs_rows, d_pre, (((0,), (0,)), ((), ())), preferred_element_type=jnp.float32
    ).astype(jnp.bfloat16)
    d_rows = lax.dot_general(
        d_pre, w_first, (((1,), (1,)), ((), ())), preferred_element_type=jnp.float32
    )
    return (expert_out, d_rows, d_first, d_second)


def to_experts(stacked):
    return lax.all_to_all(stacked, ("dp", "expert"), split_axis=1, concat_axis=1, tiled=True)


def to_sources(partials):
    return lax.all_to_all(partials, ("dp", "expert"), split_axis=0, concat_axis=0, tiled=True)


def shards(tokens, routes, combine, w_in, w_out, out_grad, head_w, labels):
    dp_size = lax.axis_size("dp")
    ex_size = lax.axis_size("expert")
    n_devices = dp_size * ex_size
    tok_rows = tokens.shape[0]
    capacity = 5 * tok_rows // 64
    share_count = n_devices // EXPERTS
    buffer_rows = EXPERTS * capacity
    flat_routes = routes.reshape(tok_rows * 2)
    route_hits = (flat_routes[:, None] == jnp.arange(EXPERTS, dtype=jnp.int32)[None, :]).astype(
        jnp.int32
    )
    earlier = jnp.cumsum(route_hits, axis=0) - route_hits
    slot_pos = jnp.sum(earlier * route_hits, axis=1)
    slot_index = flat_routes * capacity + slot_pos
    pair_table = (jnp.arange(buffer_rows, dtype=jnp.int32)[:, None] == slot_index[None, :]).astype(
        jnp.bfloat16
    )
    token_table = jnp.sum(pair_table.reshape(buffer_rows, tok_rows, 2), axis=2)
    pair_grad = (
        (combine[:, :, None] * out_grad.astype(jnp.float32)[:, None, :])
        .astype(jnp.bfloat16)
        .reshape(tok_rows * 2, D)
    )
    x_buf = jnp.dot(token_table, tokens, preferred_element_type=jnp.float32).astype(jnp.bfloat16)
    g_buf = jnp.dot(pair_table, pair_grad, preferred_element_type=jnp.float32).astype(jnp.bfloat16)
    stacked = jnp.stack([x_buf, g_buf]).reshape(2, EXPERTS, 1, capacity, D)
    stacked = jnp.broadcast_to(stacked, (2, EXPERTS, share_count, capacity, D)).reshape(
        2, n_devices, capacity, D
    )
    arrived = to_experts(stacked)
    xs_rows = arrived[0].reshape(n_devices * capacity, D)
    grad_rows = arrived[1].reshape(n_devices * capacity, D)
    expert_out, d_rows, d_w_in, d_w_out = expert_pass(xs_rows, grad_rows, w_in, w_out)
    back_out = to_sources(expert_out.reshape(n_devices, capacity, D))
    expert_sum = jnp.sum(back_out.reshape(EXPERTS, share_count, capacity, D), axis=1).reshape(
        buffer_rows, D
    )
    expert_vals = jnp.take(expert_sum, slot_index, axis=0).reshape(tok_rows, 2, D)
    mixed_out = (
        tokens.astype(jnp.float32) + jnp.sum(combine[:, :, None] * expert_vals, axis=1)
    ).astype(jnp.bfloat16)
    d_combine = jnp.sum(out_grad.astype(jnp.float32)[:, None, :] * expert_vals, axis=2)
    ex_index = lax.axis_index("expert")
    row_images = ex_size * tok_rows // PATCHES
    token_image = (ex_index * tok_rows + jnp.arange(tok_rows, dtype=jnp.int32)) // PATCHES
    image_table = (jnp.arange(row_images, dtype=jnp.int32)[:, None] == token_image[None, :]).astype(
        jnp.float32
    )
    pooled_part = jnp.dot(
        image_table, mixed_out.astype(jnp.float32), precision=lax.Precision.HIGHEST
    )
    class_cols = head_w.shape[1]
    class_ids = ex_index * class_cols + jnp.arange(class_cols, dtype=jnp.int32)
    targets = jnp.any(labels[:, :, None] == class_ids[None, None, :], axis=1).astype(jnp.float32)
    counts = lax.psum(jnp.sum(targets, axis=0), "dp")
    effective = (1.0 - beta_rate) / (1.0 - jnp.power(beta_rate, counts + 1.0))
    pooled_sum, effective_total = lax.psum((pooled_part, jnp.sum(effective)), "expert")
    back_parts = to_sources(d_rows.reshape(n_devices, capacity, D))
    back_sum = jnp.sum(back_parts.reshape(EXPERTS, share_count, capacity, D), axis=1).reshape(
        buffer_rows, D
    )
    expert_back = jnp.take(back_sum, slot_index, axis=0).reshape(tok_rows, 2, D)
    d_tokens = (out_grad.astype(jnp.float32) + jnp.sum(expert_back, axis=1)).astype(jnp.bfloat16)
    class_weight = effective * CLASSES / effective_total
    pooled = pooled_sum / PATCHES
    normed, norm_back = jax.vjp(normalize, pooled)
    normed_bf = normed.astype(jnp.bfloat16)
    logits = jnp.dot(normed_bf, head_w, preferred_element_type=jnp.float32)
    focal_terms, focal_back = jax.vjp(
        lambda logit_vals: weighted_focal(logit_vals, targets, class_weight), logits
    )
    d_logits = focal_back(jnp.ones_like(focal_terms))[0].astype(jnp.bfloat16)
    normed_part = lax.dot_general(
        d_logits, head_w, (((1,), (1,)), ((), ())), preferred_element_type=jnp.float32
    )
    d_normed, image_loss = lax.psum((normed_part, jnp.sum(focal_terms, axis=1)), "expert")
    d_pooled = norm_back(d_normed)[0]
    d_head = lax.psum_scatter(
        lax.dot_general(
            normed_bf, d_logits, (((0,), (0,)), ((), ())), preferred_element_type=jnp.float32
        ).astype(jnp.bfloat16),
        "dp",
        scatter_dimension=0,
        tiled=True,
    )
    return (mixed_out, d_tokens, d_combine, d_w_in, d_w_out, image_loss, d_pooled, d_head)


def solution(mesh):
    in_specs = (
        P(("dp", "expert"), None),
        P(("dp", "expert"), None),
        P(("dp", "expert"), None),
        P(None, ("dp", "expert")),
        P(("dp", "expert"), None),
        P(("dp", "expert"), None),
        P(None, "expert"),
        P("dp", None),
    )
    out_specs = (
        P(("dp", "expert"), None),
        P(("dp", "expert"), None),
        P(("dp", "expert"), None),
        P(None, ("dp", "expert")),
        P(("dp", "expert"), None),
        P("dp"),
        P("dp", None),
        P("dp", "expert"),
    )
    return jax.shard_map(shards, mesh=mesh, in_specs=in_specs, out_specs=out_specs, check_vma=False)
```

profile of v0, /device:TPU:0, one launch (start us, length us, event | category | flops | bytes accessed | tf_op | source)
XLA Modules:
  0.0 685.1 jit_solution(5458899573106623758)
XLA Ops:
  7.2 0.9 copy.46
  8.1 0.1 eq.78
  8.3 0.1 eq.82
  8.4 0.6 reduce-window.6
  9.0 0.2 slice_reduce_fusion.2
  9.4 0.1 reduce_sum.151
  9.5 0.8 copy.45
  10.3 0.1 mul.201
  10.5 0.7 multiply_add_fusion.1
  11.2 2.2 convolution_convert_fusion.4
  13.5 2.2 stack.9
  15.7 2.4 mul.203
  18.0 3.0 mul.204
  21.1 2.7 convolution_convert_fusion.3
  23.7 2.2 stack.10
  25.9 2.0 maximum_bitcast_fusion
  27.9 1.7 copy.51
  29.6 3.8 broadcast_in_dim.16
  33.5 89.6 %all_to_all.15 = bf16[2,128,10,1280]{3,0,2,1:T(2,128)(2,1)S(1)} all-to-all(bf16[2,128,10,1280]{3,0,2,1:T(2,128)(2,1)S(1)} %bitcast.42), channel_id=1, replica_groups=mesh['dp'=16,'expert'=8] {'dp','expert'}, dimensions={1} | all-to-all | bytes 13107200 | tf_op jit(solution)/shard_map/all_to_all | solution.py:53
  123.1 40.3 %slice_reduce_fusion = (bf16[128,10,1280]{2,1,0:T(8,128)(2,1)}, bf16[128,10,1280]{2,1,0:T(8,128)(2,1)}) fusion(bf16[2,128,10,1280]{3,0,2,1:T(2,128)(2,1)S(1)} %all_to_all.15), kind=kLoop, calls=%fused_computation.16 | loop fusion | bytes 13107200 | tf_op jit(solution)/shard_map/slice | solution.py:92
  163.4 7.0 %reshape_squeeze.7 = bf16[1280,1280]{1,0:T(8,128)(2,1)} reshape(bf16[128,10,1280]{2,1,0:T(8,128)(2,1)} %get-tuple-element.49) | data formatting | bytes 6553600 | tf_op jit(solution)/shard_map/reshape;squeeze | solution.py:92
  170.4 7.0 %reshape_squeeze.6 = bf16[1280,1280]{1,0:T(8,128)(2,1)} reshape(bf16[128,10,1280]{2,1,0:T(8,128)(2,1)} %get-tuple-element.50) | data formatting | bytes 6553600 | tf_op jit(solution)/shard_map/reshape;squeeze | solution.py:91
  177.4 7.6 %fusion.37 = f32[1280,1280]{1,0:T(8,128)S(1)} fusion(bf16[1280,1280]{1,0:T(8,128)(2,1)} %reshape_squeeze.7, bf16[1280,1280]{1,0:T(8,128)(2,1)} %param.15), kind=kOutput, calls=%fused_computation.102 | convolution fusion | flops 4194304000 | bytes 13107200 | tf_op jit(solution)/shard_map/dot_general | solution.py:36
  185.0 9.4 %fusion.6 = (bf16[1280,1280]{1,0:T(8,128)(2,1)S(1)}, f32[1280,1280]{1,0:T(8,128)}) fusion(f32[1280,1280]{1,0:T(8,128)S(1)} %fusion.37, bf16[1280,1280]{1,0:T(8,128)(2,1)S(1)} %copy-done.4, bf16[1280,1280]{1,0:T(8,128)(2,1)S(1)} %copy-done), kind=kOutput, calls=%fused_computation.15 | convolution fusion | flops 4227072000 | bytes 22937600 | tf_op jit(solution)/shard_map/dot_general | solution.py:32
  194.4 1.8 copy-done.10
  196.2 6.5 fusion.38
  202.8 8.6 %reshape.154 = f32[128,10,1280]{2,1,0:T(8,128)} reshape(f32[1280,1280]{1,0:T(8,128)} %fusion.38) | data formatting | bytes 13107200 | tf_op jit(solution)/shard_map/reshape | solution.py:118
  211.4 6.3 all-to-all-start.2
  217.7 11.2 %fusion.36 = f32[1280,1280]{1,0:T(8,128)} fusion(bf16[1280,1280]{1,0:T(8,128)(2,1)S(1)} %copy-done.9, f32[1280,1280]{1,0:T(8,128)} %get-tuple-element.63), kind=kOutput, calls=%fused_computation.101 | convolution fusion | flops 4209049600 | bytes 16384000 | tf_op jit(solution)/shard_map/dot_general | solution.py:35
  228.9 8.6 %reshape.150 = f32[128,10,1280]{2,1,0:T(8,128)} reshape(f32[1280,1280]{1,0:T(8,128)} %fusion.36) | data formatting | bytes 13107200 | tf_op jit(solution)/shard_map/reshape | solution.py:94
  237.5 103.3 %all-to-all-done.2 = f32[128,10,1280]{2,1,0:T(8,128)} async-done(((f32[128,10,1280]{2,1,0:T(8,128)}), f32[128,10,1280]{2,1,0:T(8,128)}, u32[]{:S(2)}, u32[]{:S(2)}) %all-to-all-start.2) | async-done | bytes 6553632 | tf_op jit(solution)/shard_map/all_to_all | solution.py:57
  340.8 10.3 %all-to-all-start.1 = ((f32[128,10,1280]{2,1,0:T(8,128)}), f32[128,10,1280]{2,1,0:T(8,128)}, u32[]{:S(2)}, u32[]{:S(2)}) async-start(f32[128,10,1280]{2,1,0:T(8,128)} %reshape.150), calls=%async_computation.1 | async-start | bytes 20971520 | tf_op jit(solution)/shard_map/all_to_all | solution.py:57
  351.1 0.2 compare_reduce_fusion
  351.4 183.0 %psum.35 = f32[2176]{0:T(1024)S(1)} all-reduce(f32[2176]{0:T(1024)S(1)} %convert_reduce_fusion), channel_id=1, replica_groups=mesh['dp'=16,'expert'=8] {'dp'}, use_global_device_ids=true, to_apply=%region_11.13 | all-reduce | flops 2176 | bytes 17408 | tf_op jit(solution)/shard_map/psum | solution.py:115
  534.4 0.6 fusion.28
  535.0 6.8 bitcast_reduce_fusion
  541.8 1.8 reshape.156
  543.7 6.8 bitcast_reduce_fusion.1
  550.5 1.8 reshape.152
  552.4 2.2 gather_fusion.1
  554.6 2.3 gather_fusion
  556.9 3.1 multiply_reduce_fusion
  560.0 0.8 reshape.153
  560.8 1.6 multiply_reduce_fusion.1
  562.5 0.2 fusion.29
  562.6 27.7 %all-reduce.2 = (f32[4,1280]{1,0:T(4,128)S(1)}, f32[]{:T(128)}) all-reduce(f32[4,1280]{1,0:T(4,128)S(1)} %fusion.29, f32[]{:T(128)} %fusion.28), channel_id=1, replica_groups=mesh['dp'=16,'expert'=8] {'expert'}, use_global_device_ids=true, to_apply=%region_14.16 | all-reduce | flops 5121 | bytes 40968 | tf_op jit(solution)/shard_map/psum | solution.py:117
  590.3 0.7 multiply_divide_fusion
  591.1 0.2 multiply_reduce_fusion.4
  591.3 3.6 multiply_reduce_fusion.2
  595.0 4.1 convolution_convert_fusion
  599.1 1.9 copy-done.5
  601.0 8.2 %convolution_convert_fusion.2 = bf16[1280,1280]{1,0:T(8,128)(2,1)} fusion(bf16[1280,1280]{1,0:T(8,128)(2,1)S(1)} %copy-done.5, bf16[1280,1280]{1,0:T(8,128)(2,1)} %copy-done.10), kind=kOutput, calls=%fused_computation.8 | convolution fusion | flops 4195942400 | bytes 9830400 | tf_op jit(solution)/shard_map/dot_general | solution.py:43
  609.2 10.1 %convolution_convert_fusion.1 = bf16[1280,1280]{1,0:T(8,128)(2,1)} fusion(bf16[1280,1280]{1,0:T(8,128)(2,1)S(1)} %copy-done.3, f32[1280,1280]{1,0:T(8,128)} %get-tuple-element.63), kind=kOutput, calls=%fused_computation.7 | convolution fusion | flops 4210688000 | bytes 13107200 | tf_op jit(solution)/shard_map/dot_general | solution.py:40
  619.4 1.6 fusion.34
  620.9 25.1 %all-reduce.1 = (f32[4]{0:T(128)}, f32[4,1280]{1,0:T(4,128)S(1)}) all-reduce(f32[4]{0:T(128)S(1)} %get-tuple-element.64, f32[4,1280]{1,0:T(4,128)S(1)} %fusion.34), channel_id=1, replica_groups=mesh['dp'=16,'expert'=8] {'expert'}, use_global_device_ids=true, to_apply=%region_18.21 | all-reduce | flops 5124 | bytes 40992 | tf_op jit(solution)/shard_map/psum | solution.py:136
  646.0 0.1 reduce_sum.158
  646.1 0.6 copy.52
  646.8 3.0 reshape.157
  649.8 3.7 reduce_sum.156
  653.5 0.2 multiply_reduce_fusion.6
  653.7 0.2 multiply_reduce_fusion.5
  653.9 0.7 add_add_fusion
  654.6 1.9 add_convert_fusion
  656.6 21.2 %reduce-scatter.4.cloned.1.call-done = bf16[80,2176]{1,0:T(8,128)(2,1)} async-done(((bf16[1280,2176]{1,0:T(8,128)(2,1)}), bf16[80,2176]{1,0:T(8,128)(2,1)}) %reduce-scatter.4.cloned.1.call-update) | async-done | bytes 348176
  (46 shorter events, 0.6 us)
Async XLA Ops:
  7.2 177.8 %copy-start = (bf16[1280,1280]{1,0:T(8,128)(2,1)S(1)}, bf16[1280,1280]{1,0:T(8,128)(2,1)}, u32[]{:S(2)}) copy-start(bf16[1280,1280]{1,0:T(8,128)(2,1)} %param.14) | copy-start | bytes 9830404
  177.4 7.6 %copy-start.4 = (bf16[1280,1280]{1,0:T(8,128)(2,1)S(1)}, bf16[1280,1280]{1,0:T(8,128)(2,1)}, u32[]{:S(2)}) copy-start(bf16[1280,1280]{1,0:T(8,128)(2,1)} %reshape_squeeze.6) | copy-start | bytes 9830404
  194.4 1.8 copy-start.10
  211.4 6.3 copy-start.9
  211.4 129.4 %all-to-all-start.2 = ((f32[128,10,1280]{2,1,0:T(8,128)}), f32[128,10,1280]{2,1,0:T(8,128)}, u32[]{:S(2)}, u32[]{:S(2)}) async-start(f32[128,10,1280]{2,1,0:T(8,128)} %reshape.154), calls=%async_computation.2 | async-start | bytes 20971520 | tf_op jit(solution)/shard_map/all_to_all | solution.py:57
  237.5 113.6 %copy-start.8 = (s32[4,4]{1,0:T(4,128)S(1)}, s32[4,4]{1,0:T(4,128)}, u32[]{:S(2)}) copy-start(s32[4,4]{1,0:T(4,128)} %param.18) | copy-start | bytes 196
  340.8 202.9 %all-to-all-start.1 = ((f32[128,10,1280]{2,1,0:T(8,128)}), f32[128,10,1280]{2,1,0:T(8,128)}, u32[]{:S(2)}, u32[]{:S(2)}) async-start(f32[128,10,1280]{2,1,0:T(8,128)} %reshape.150), calls=%async_computation.1 | async-start | bytes 20971520 | tf_op jit(solution)/shard_map/all_to_all | solution.py:57
  351.1 326.7 %reduce-scatter.4.cloned.1.call-start = ((), (), s32[]{:S(2)}) async-start(), calls=%async_computation.4 | async-start | bytes 5918720
  554.6 2.3 copy-start.2
  556.9 5.5 copy-start.7
  562.5 32.5 %copy-start.6 = (bf16[128,1280]{1,0:T(8,128)(2,1)}, bf16[128,1280]{1,0:T(8,128)(2,1)S(1)}, u32[]{:S(2)}) copy-start(bf16[128,1280]{1,0:T(8,128)(2,1)S(1)} %add_convert_fusion.1) | copy-start | bytes 983044
  599.1 1.9 copy-start.5
  601.0 8.2 %copy-start.3 = (bf16[1280,1280]{1,0:T(8,128)(2,1)S(1)}, bf16[1280,1280]{1,0:T(8,128)(2,1)}, u32[]{:S(2)}) copy-start(bf16[1280,1280]{1,0:T(8,128)(2,1)} %reshape_squeeze.7) | copy-start | bytes 9830404
  601.0 18.3 %slice-start = ((s8[5570560]{0:T(1024)(128)(4,1)}), s8[4194304]{0:T(1024)(128)(4,1)S(1)}, s32[]{:S(2)}) async-start(s8[5570560]{0:T(1024)(128)(4,1)} %bitcast.43), calls=%async_computation.5 | async-start | bytes 8388608
  609.2 10.1 %slice-start.1 = ((s8[5570560]{0:T(1024)(128)(4,1)}), s8[1376256]{0:T(1024)(128)(4,1)S(1)}, s32[]{:S(2)}) async-start(s8[5570560]{0:T(1024)(128)(4,1)} %bitcast.43), calls=%async_computation.6 | async-start | bytes 2752512
  609.2 68.5 %copy-start.1 = (bf16[1280,1280]{1,0:T(8,128)(2,1)S(1)}, bf16[1280,1280]{1,0:T(8,128)(2,1)}, u32[]{:S(2)}) copy-start(bf16[1280,1280]{1,0:T(8,128)(2,1)} %param.14) | copy-start | bytes 9830404
Sparse Core Ops, SparseCore 0:
  599.2 78.4 reduce-scatter.3
where the time goes:
time: 692 us; the launch traced here: 685 us
  blocking collectives  325 us (47%)
  waiting for transfers between devices  124 us (18%)
  local copies, waits for them, and re-layouts  106 us (15%)
  matrix products  67.4 us (10%)
  other arithmetic  30.6 us (4%)
  starting transfers between devices  16.6 us (2%)
  between operations  14.8 us (2%)
    psum x1, blocking collectives, shards(): counts = lax.psum(jnp.sum(targets, axis=0), 'dp')  183 us
    all_to_all x2, waiting for transfers between devices, to_sources(): lax.all_to_all(partials, ('dp', 'expert'), split_axis=0, concat_axis=0, t...  103 us
    all_to_all x1, blocking collectives, to_experts(): lax.all_to_all(stacked, ('dp', 'expert'), split_axis=1, concat_axis=1, ti...  89.6 us
    slice x1, local copies, waits for them, and re-layouts, shards(): grad_rows = arrived[1].reshape(n_devices * capacity, D)  40.3 us
    psum x1, blocking collectives, shards(): lax.psum((pooled_part, jnp.sum(effective)), 'expert')  27.7 us
    psum x1, blocking collectives, shards(): lax.psum((normed_part, jnp.sum(focal_terms, axis=1)), 'expert')  25.1 us
    unnamed x2, waiting for transfers between devices  21.2 us
    all_to_all x2, starting transfers between devices, to_sources(): lax.all_to_all(partials, ('dp', 'expert'), split_axis=0, concat_axis=0, t...  16.5 us
  transfers between devices with their start and end apart: 3, of which 2 were waited for; matrix products, arithmetic and copies ran while one was open for 9% of the time, Pallas kernels for 0%

commit v1 on v0

--- a/solution.py
+++ b/solution.py
@@ -112,7 +112,7 @@
     class_cols = head_w.shape[1]
     class_ids = ex_index * class_cols + jnp.arange(class_cols, dtype=jnp.int32)
     targets = jnp.any(labels[:, :, None] == class_ids[None, None, :], axis=1).astype(jnp.float32)
-    counts = lax.psum(jnp.sum(targets, axis=0), "dp")
+    counts = jnp.sum(lax.all_gather(jnp.sum(targets, axis=0), "dp"), axis=0)
     effective = (1.0 - beta_rate) / (1.0 - jnp.power(beta_rate, counts + 1.0))
     pooled_sum, effective_total = lax.psum((pooled_part, jnp.sum(effective)), "expert")
     back_parts = to_sources(d_rows.reshape(n_devices, capacity, D))

time: 692 us -> 649 us (0.938)
  blocking collectives: 325 us -> 279 us
    psum x1 -> x0, blocking collectives: 183 us -> none  [shards(): counts = lax.psum(jnp.sum(targets, axis=0), 'dp')]
    all_gather x0 -> x1, blocking collectives: none -> 136 us  [shards(): counts = jnp.sum(lax.all_gather(jnp.sum(targets, axis=0), 'dp'), axis=0)]
where the time goes in v1:
time: 649 us; the launch traced here: 643 us
  blocking collectives  279 us (43%)
  waiting for transfers between devices  129 us (20%)
  local copies, waits for them, and re-layouts  106 us (16%)
  matrix products  67.1 us (10%)
  other arithmetic  30.7 us (5%)
  starting transfers between devices  16.6 us (3%)
  between operations  14.8 us (2%)
    all_gather x1, blocking collectives, shards(): counts = jnp.sum(lax.all_gather(jnp.sum(targets, axis=0), 'dp'), axis=0)  136 us
    all_to_all x2, waiting for transfers between devices, to_sources(): lax.all_to_all(partials, ('dp', 'expert'), split_axis=0, concat_axis=0, t...  103 us
    all_to_all x1, blocking collectives, to_experts(): lax.all_to_all(stacked, ('dp', 'expert'), split_axis=1, concat_axis=1, ti...  89.6 us
    slice x1, local copies, waits for them, and re-layouts, shards(): grad_rows = arrived[1].reshape(n_devices * capacity, D)  40.3 us
    psum x1, blocking collectives, shards(): lax.psum((pooled_part, jnp.sum(effective)), 'expert')  27.7 us
    unnamed x2, waiting for transfers between devices  25.7 us
    psum x1, blocking collectives, shards(): lax.psum((normed_part, jnp.sum(focal_terms, axis=1)), 'expert')  25.2 us
    all_to_all x2, starting transfers between devices, to_sources(): lax.all_to_all(partials, ('dp', 'expert'), split_axis=0, concat_axis=0, t...  16.5 us
  transfers between devices with their start and end apart: 3, of which 2 were waited for; matrix products, arithmetic and copies ran while one was open for 9% of the time, Pallas kernels for 0%

profile of v1, /device:TPU:0, one launch (start us, length us, event | category | flops | bytes accessed | tf_op | source)
XLA Modules:
  0.0 642.6 jit_solution(10079464533597648352)
XLA Ops:
  7.2 0.9 copy.46
  8.1 0.1 eq.78
  8.3 0.1 eq.82
  8.4 0.6 reduce-window.6
  9.0 0.2 slice_reduce_fusion.2
  9.4 0.1 reduce_sum.160
  9.5 0.8 copy.45
  10.3 0.1 mul.205
  10.5 0.7 multiply_add_fusion.1
  11.2 2.2 convolution_convert_fusion.4
  13.5 2.2 stack.9
  15.7 2.4 mul.207
  18.0 3.0 mul.208
  21.1 2.7 convolution_convert_fusion.3
  23.7 2.2 stack.10
  25.9 2.0 maximum_bitcast_fusion
  27.9 1.7 copy.51
  29.6 3.8 broadcast_in_dim.16
  33.5 89.6 %all_to_all.15 = bf16[2,128,10,1280]{3,0,2,1:T(2,128)(2,1)S(1)} all-to-all(bf16[2,128,10,1280]{3,0,2,1:T(2,128)(2,1)S(1)} %bitcast.42), channel_id=1, replica_groups=mesh['dp'=16,'expert'=8] {'dp','expert'}, dimensions={1} | all-to-all | bytes 13107200 | tf_op jit(solution)/shard_map/all_to_all | solution.py:53
  123.1 40.3 %slice_reduce_fusion = (bf16[128,10,1280]{2,1,0:T(8,128)(2,1)}, bf16[128,10,1280]{2,1,0:T(8,128)(2,1)}) fusion(bf16[2,128,10,1280]{3,0,2,1:T(2,128)(2,1)S(1)} %all_to_all.15), kind=kLoop, calls=%fused_computation.16 | loop fusion | bytes 13107200 | tf_op jit(solution)/shard_map/slice | solution.py:92
  163.4 7.0 %reshape_squeeze.7 = bf16[1280,1280]{1,0:T(8,128)(2,1)} reshape(bf16[128,10,1280]{2,1,0:T(8,128)(2,1)} %get-tuple-element.49) | data formatting | bytes 6553600 | tf_op jit(solution)/shard_map/reshape;squeeze | solution.py:92
  170.4 7.0 %reshape_squeeze.6 = bf16[1280,1280]{1,0:T(8,128)(2,1)} reshape(bf16[128,10,1280]{2,1,0:T(8,128)(2,1)} %get-tuple-element.50) | data formatting | bytes 6553600 | tf_op jit(solution)/shard_map/reshape;squeeze | solution.py:91
  177.4 7.6 %fusion.37 = f32[1280,1280]{1,0:T(8,128)S(1)} fusion(bf16[1280,1280]{1,0:T(8,128)(2,1)} %reshape_squeeze.7, bf16[1280,1280]{1,0:T(8,128)(2,1)} %param.15), kind=kOutput, calls=%fused_computation.102 | convolution fusion | flops 4194304000 | bytes 13107200 | tf_op jit(solution)/shard_map/dot_general | solution.py:36
  185.0 9.4 %fusion.6 = (bf16[1280,1280]{1,0:T(8,128)(2,1)S(1)}, f32[1280,1280]{1,0:T(8,128)}) fusion(f32[1280,1280]{1,0:T(8,128)S(1)} %fusion.37, bf16[1280,1280]{1,0:T(8,128)(2,1)S(1)} %copy-done.4, bf16[1280,1280]{1,0:T(8,128)(2,1)S(1)} %copy-done), kind=kOutput, calls=%fused_computation.15 | convolution fusion | flops 4227072000 | bytes 22937600 | tf_op jit(solution)/shard_map/dot_general | solution.py:32
  194.4 1.8 copy-done.10
  196.2 6.5 %fusion.38 = f32[1280,1280]{1,0:T(8,128)} fusion(bf16[1280,1280]{1,0:T(8,128)(2,1)S(1)} %get-tuple-element.62, bf16[1280,1280]{1,0:T(8,128)(2,1)S(1)} %copy-done), kind=kOutput, calls=%fused_computation.103 | convolution fusion | flops 4194304000 | bytes 13107200 | tf_op jit(solution)/shard_map/dot_general | solution.py:46
  202.8 8.6 %reshape.161 = f32[128,10,1280]{2,1,0:T(8,128)} reshape(f32[1280,1280]{1,0:T(8,128)} %fusion.38) | data formatting | bytes 13107200 | tf_op jit(solution)/shard_map/reshape | solution.py:118
  211.4 6.3 all-to-all-start.2
  217.7 11.2 %fusion.36 = f32[1280,1280]{1,0:T(8,128)} fusion(bf16[1280,1280]{1,0:T(8,128)(2,1)S(1)} %copy-done.9, f32[1280,1280]{1,0:T(8,128)} %get-tuple-element.63), kind=kOutput, calls=%fused_computation.101 | convolution fusion | flops 4209049600 | bytes 16384000 | tf_op jit(solution)/shard_map/dot_general | solution.py:35
  228.9 8.6 %reshape.157 = f32[128,10,1280]{2,1,0:T(8,128)} reshape(f32[1280,1280]{1,0:T(8,128)} %fusion.36) | data formatting | bytes 13107200 | tf_op jit(solution)/shard_map/reshape | solution.py:94
  237.5 103.3 %all-to-all-done.2 = f32[128,10,1280]{2,1,0:T(8,128)} async-done(((f32[128,10,1280]{2,1,0:T(8,128)}), f32[128,10,1280]{2,1,0:T(8,128)}, u32[]{:S(2)}, u32[]{:S(2)}) %all-to-all-start.2) | async-done | bytes 6553632 | tf_op jit(solution)/shard_map/all_to_all | solution.py:57
  340.8 10.3 %all-to-all-start.1 = ((f32[128,10,1280]{2,1,0:T(8,128)}), f32[128,10,1280]{2,1,0:T(8,128)}, u32[]{:S(2)}, u32[]{:S(2)}) async-start(f32[128,10,1280]{2,1,0:T(8,128)} %reshape.157), calls=%async_computation.1 | async-start | bytes 20971520 | tf_op jit(solution)/shard_map/all_to_all | solution.py:57
  351.1 0.2 compare_reduce_fusion
  351.4 136.0 %all-gather.1 = f32[16,1,2176]{2,1,0:T(1,128)S(1)} all-gather(f32[1,1,2176]{2,1,0:T(1,128)S(1)} %reshape.184), channel_id=2, replica_groups=mesh['dp'=16,'expert'=8] {'dp'}, dimensions={0}, use_global_device_ids=true | all-gather | bytes 147968 | tf_op jit(solution)/shard_map/all_gather | solution.py:115
  487.5 0.6 fusion.28
  488.1 6.8 %bitcast_reduce_fusion = f32[32,10,1280]{2,1,0:T(8,128)} fusion(f32[128,10,1280]{2,1,0:T(8,128)} %all-to-all-done.2), kind=kLoop, calls=%fused_computation.3 | loop fusion | flops 1228800 | bytes 8192000 | tf_op jit(solution)/shard_map/reduce_sum | solution.py:119
  495.0 1.8 reshape.163
  496.8 6.8 %bitcast_reduce_fusion.1 = f32[32,10,1280]{2,1,0:T(8,128)} fusion(f32[128,10,1280]{2,1,0:T(8,128)} %all-to-all-done.1), kind=kLoop, calls=%fused_computation.4 | loop fusion | flops 1228800 | bytes 8192000 | tf_op jit(solution)/shard_map/reduce_sum | solution.py:95
  503.7 1.8 reshape.159
  505.5 2.2 gather_fusion.1
  507.8 2.3 gather_fusion
  510.0 3.1 multiply_reduce_fusion
  513.1 0.8 reshape.160
  513.9 1.6 multiply_reduce_fusion.1
  515.6 0.2 fusion.29
  515.8 27.7 %all-reduce.2 = (f32[4,1280]{1,0:T(4,128)S(1)}, f32[]{:T(128)}) all-reduce(f32[4,1280]{1,0:T(4,128)S(1)} %fusion.29, f32[]{:T(128)} %fusion.28), channel_id=1, replica_groups=mesh['dp'=16,'expert'=8] {'expert'}, use_global_device_ids=true, to_apply=%region_14.16 | all-reduce | flops 5121 | bytes 40968 | tf_op jit(solution)/shard_map/psum | solution.py:117
  543.5 0.7 multiply_divide_fusion
  544.3 0.2 multiply_reduce_fusion.4
  544.5 3.6 multiply_reduce_fusion.2
  548.1 4.1 convolution_convert_fusion
  552.3 1.9 copy-done.5
  554.2 8.0 %convolution_convert_fusion.2 = bf16[1280,1280]{1,0:T(8,128)(2,1)} fusion(bf16[1280,1280]{1,0:T(8,128)(2,1)S(1)} %copy-done.5, bf16[1280,1280]{1,0:T(8,128)(2,1)} %copy-done.10), kind=kOutput, calls=%fused_computation.8 | convolution fusion | flops 4195942400 | bytes 9830400 | tf_op jit(solution)/shard_map/dot_general | solution.py:43
  562.2 10.1 %convolution_convert_fusion.1 = bf16[1280,1280]{1,0:T(8,128)(2,1)} fusion(bf16[1280,1280]{1,0:T(8,128)(2,1)S(1)} %copy-done.3, f32[1280,1280]{1,0:T(8,128)} %get-tuple-element.63), kind=kOutput, calls=%fused_computation.7 | convolution fusion | flops 4210688000 | bytes 13107200 | tf_op jit(solution)/shard_map/dot_general | solution.py:40
  572.3 1.6 fusion.34
  573.9 25.2 %all-reduce.1 = (f32[4]{0:T(128)}, f32[4,1280]{1,0:T(4,128)S(1)}) all-reduce(f32[4]{0:T(128)S(1)} %get-tuple-element.64, f32[4,1280]{1,0:T(4,128)S(1)} %fusion.34), channel_id=1, replica_groups=mesh['dp'=16,'expert'=8] {'expert'}, use_global_device_ids=true, to_apply=%region_18.21 | all-reduce | flops 5124 | bytes 40992 | tf_op jit(solution)/shard_map/psum | solution.py:136
  599.0 0.1 reduce_sum.167
  599.2 0.6 copy.52
  599.8 3.0 reshape.164
  602.8 3.7 reduce_sum.165
  606.5 0.2 multiply_reduce_fusion.6
  606.8 0.2 multiply_reduce_fusion.5
  607.0 0.7 add_add_fusion
  607.7 2.0 add_convert_fusion
  609.7 25.7 %reduce-scatter.4.cloned.1.call-done = bf16[80,2176]{1,0:T(8,128)(2,1)} async-done(((bf16[1280,2176]{1,0:T(8,128)(2,1)}), bf16[80,2176]{1,0:T(8,128)(2,1)}) %reduce-scatter.4.cloned.1.call-update) | async-done | bytes 348176
  (48 shorter events, 0.8 us)
Async XLA Ops:
  7.2 177.8 %copy-start = (bf16[1280,1280]{1,0:T(8,128)(2,1)S(1)}, bf16[1280,1280]{1,0:T(8,128)(2,1)}, u32[]{:S(2)}) copy-start(bf16[1280,1280]{1,0:T(8,128)(2,1)} %param.14) | copy-start | bytes 9830404
  177.4 7.6 %copy-start.4 = (bf16[1280,1280]{1,0:T(8,128)(2,1)S(1)}, bf16[1280,1280]{1,0:T(8,128)(2,1)}, u32[]{:S(2)}) copy-start(bf16[1280,1280]{1,0:T(8,128)(2,1)} %reshape_squeeze.6) | copy-start | bytes 9830404
  194.4 1.8 copy-start.10
  211.4 6.3 copy-start.9
  211.4 129.4 %all-to-all-start.2 = ((f32[128,10,1280]{2,1,0:T(8,128)}), f32[128,10,1280]{2,1,0:T(8,128)}, u32[]{:S(2)}, u32[]{:S(2)}) async-start(f32[128,10,1280]{2,1,0:T(8,128)} %reshape.161), calls=%async_computation.2 | async-start | bytes 20971520 | tf_op jit(solution)/shard_map/all_to_all | solution.py:57
  237.5 113.6 %copy-start.8 = (s32[4,4]{1,0:T(4,128)S(1)}, s32[4,4]{1,0:T(4,128)}, u32[]{:S(2)}) copy-start(s32[4,4]{1,0:T(4,128)} %param.18) | copy-start | bytes 196
  340.8 156.0 %all-to-all-start.1 = ((f32[128,10,1280]{2,1,0:T(8,128)}), f32[128,10,1280]{2,1,0:T(8,128)}, u32[]{:S(2)}, u32[]{:S(2)}) async-start(f32[128,10,1280]{2,1,0:T(8,128)} %reshape.157), calls=%async_computation.1 | async-start | bytes 20971520 | tf_op jit(solution)/shard_map/all_to_all | solution.py:57
  351.1 284.3 %reduce-scatter.4.cloned.1.call-start = ((), (), s32[]{:S(2)}) async-start(), calls=%async_computation.4 | async-start | bytes 5918720
  507.8 2.3 copy-start.2
  510.0 5.5 copy-start.7
  515.6 32.5 %copy-start.6 = (bf16[128,1280]{1,0:T(8,128)(2,1)}, bf16[128,1280]{1,0:T(8,128)(2,1)S(1)}, u32[]{:S(2)}) copy-start(bf16[128,1280]{1,0:T(8,128)(2,1)S(1)} %add_convert_fusion.1) | copy-start | bytes 983044
  552.3 1.9 copy-start.5
  554.2 8.0 %copy-start.3 = (bf16[1280,1280]{1,0:T(8,128)(2,1)S(1)}, bf16[1280,1280]{1,0:T(8,128)(2,1)}, u32[]{:S(2)}) copy-start(bf16[1280,1280]{1,0:T(8,128)(2,1)} %reshape_squeeze.7) | copy-start | bytes 9830404
  554.2 18.1 %slice-start = ((s8[5570560]{0:T(1024)(128)(4,1)}), s8[4194304]{0:T(1024)(128)(4,1)S(1)}, s32[]{:S(2)}) async-start(s8[5570560]{0:T(1024)(128)(4,1)} %bitcast.43), calls=%async_computation.5 | async-start | bytes 8388608
  562.2 10.1 %slice-start.1 = ((s8[5570560]{0:T(1024)(128)(4,1)}), s8[1376256]{0:T(1024)(128)(4,1)S(1)}, s32[]{:S(2)}) async-start(s8[5570560]{0:T(1024)(128)(4,1)} %bitcast.43), calls=%async_computation.6 | async-start | bytes 2752512
  562.2 73.1 %copy-start.1 = (bf16[1280,1280]{1,0:T(8,128)(2,1)S(1)}, bf16[1280,1280]{1,0:T(8,128)(2,1)}, u32[]{:S(2)}) copy-start(bf16[1280,1280]{1,0:T(8,128)(2,1)} %param.14) | copy-start | bytes 9830404
Sparse Core Ops, SparseCore 0:
  552.4 82.8 reduce-scatter.3
